TPU v7x, 32 devices: a whole 2x2x4 slice. The times are simulated.
32 devices in a mesh: prow: 4 (over z), pcol: 8 (over y, x, core).
Axes of the slice: x: 2, y: 2, z: 4, core: 2. Of those that a mesh axis runs over, the one named last changes fastest.
Arguments:
- ainv_in: float32 [36, 4, 18, 8, 128, 128], P(None, 'prow', None, 'pcol'), as said below
- ufactor: bfloat16 [36, 4, 6, 128, 128], P(None, 'prow'), may hold values from -0.08984375 to 0.08984375
- dinv: float32 [6, 128, 128], replicated, may hold values from -6 to 6
- pattern: int32 [144, 144], replicated, may hold values from 0 to 1, as said below
Outputs:
- ainv_out: float32 [36, 4, 18, 8, 128, 128], P(None, 'prow', None, 'pcol')
Inputs may be any that keep to these rules, and one draw needn't show every extreme that they name: For a column j below 6, pattern[i, j] is 0 for i <= j, 1 at the parent row (the nearest row below j that has a 1, at most 3 below j), and the other 1s of column j lie in rows where the parent's column has a 1; for j at least 6, pattern[i, j] is 1 exactly where i > j. `ainv_in`: a symmetric matrix.
All inputs are finite; a program needn't handle non-finite values.
Results may differ from a plain program's by a relative error of at most 0.0003.
Values may be sent and summed in bfloat16 or wider, within the bound.
A program may use at most 192 MiB of HBM per device.

v0:
```python
import jax
import jax.numpy as jnp
from jax import lax
from jax.sharding import PartitionSpec as P


def spread(value, axis, source):
    kept = jnp.where(lax.axis_index(axis) == source, value, 0).astype(value.dtype)
    return lax.psum(kept, axis)


def per_device(ainv_in, ufactor, dinv, pattern):
    row_blocks, _, col_blocks, _, width, _ = ainv_in.shape
    step_count = dinv.shape[0]
    blocks = ainv_in.reshape(row_blocks, col_blocks, width, width)
    lower = ufactor.reshape(row_blocks, step_count, width, width)
    row_count = lax.axis_size("prow")
    col_count = lax.axis_size("pcol")
    prow_id = lax.axis_index("prow")
    pcol_id = lax.axis_index("pcol")
    row_ids = jnp.arange(row_blocks, dtype=jnp.int32) * row_count + prow_id
    col_ids = jnp.arange(col_blocks, dtype=jnp.int32) * col_count + pcol_id
    fold_ratio = col_count // row_count
    pick_slot = pcol_id // row_count
    home_row = pcol_id % row_count
    mask_rows = pattern[row_ids, :]
    live_lower = mask_rows[:, :step_count] > 0
    masked_lower = jnp.where(live_lower[:, :, None, None], lower, jnp.zeros_like(lower))
    chosen_cols = lax.dynamic_index_in_dim(
        masked_lower.reshape(col_blocks, fold_ratio, step_count, width, width),
        pick_slot,
        1,
        keepdims=False,
    )
    other_cols = spread(chosen_cols, "prow", home_row)

    def fetch(column):
        own_col = lax.dynamic_index_in_dim(masked_lower, column, 1, keepdims=False)
        other_rows = lax.dynamic_index_in_dim(other_cols, column, 1, keepdims=False)
        return (own_col, other_rows)

    def advance(taken, matrix):
        column = step_count - 1 - taken
        own_col, other_rows = fetch(column)
        partial_value = -jnp.einsum(
            "acxy,cyz->axz", matrix, other_rows.astype(jnp.float32), precision=lax.Precision.HIGHEST
        )
        col_piece = lax.psum_scatter(partial_value, "pcol", scatter_dimension=1, tiled=True)
        col_whole = lax.all_gather(col_piece, "pcol", axis=1, tiled=True)
        live_rows = lax.dynamic_index_in_dim(mask_rows, column, 1, keepdims=False) > 0
        inverse_col = jnp.where(live_rows[:, None, None], col_whole, jnp.zeros_like(col_whole))
        diag_term = jnp.einsum(
            "axy,axz->yz", own_col.astype(jnp.float32), inverse_col, precision=lax.Precision.HIGHEST
        )
        diag_total = lax.psum(diag_term, "prow")
        diag_block = lax.dynamic_index_in_dim(dinv, column, 0, keepdims=False) - diag_total
        new_col = jnp.where((row_ids == column)[:, None, None], diag_block[None], inverse_col)
        col_slot = column // col_count
        old_col = lax.dynamic_index_in_dim(matrix, col_slot, 1, keepdims=False)
        matrix = lax.dynamic_update_index_in_dim(
            matrix, jnp.where(pcol_id == column % col_count, new_col, old_col), col_slot, 1
        )
        chosen = lax.dynamic_index_in_dim(
            inverse_col.reshape(col_blocks, fold_ratio, width, width), pick_slot, 1, keepdims=False
        )
        across = spread(chosen, "prow", home_row)
        row_vals = jnp.where((col_ids == column)[:, None, None], diag_block[None], across)
        row_vals = jnp.swapaxes(row_vals, 1, 2)
        row_slot = column // row_count
        old_row = lax.dynamic_index_in_dim(matrix, row_slot, 0, keepdims=False)
        matrix = lax.dynamic_update_index_in_dim(
            matrix, jnp.where(prow_id == column % row_count, row_vals, old_row), row_slot, 0
        )
        return matrix

    blocks = lax.fori_loop(0, step_count, advance, blocks)
    return blocks.reshape(ainv_in.shape)


def solution(mesh):
    placed = (
        P(None, "prow", None, "pcol", None, None),
        P(None, "prow", None, None, None),
        P(),
        P(),
    )
    return jax.shard_map(
        per_device,
        mesh=mesh,
        in_specs=placed,
        out_specs=P(None, "prow", None, "pcol", None, None),
        check_vma=False,
    )
```

profile of v0, /device:TPU:0, one launch (start us, length us, event | category | flops | bytes accessed | tf_op | source)
XLA Modules:
  0.0 1241.6 jit_solution(2986418367816600455)
XLA Ops:
  6.5 30.5 %copy.57 = f32[36,1,18,1,128,128]{5,4,3,2,1,0:T(8,128)} copy(f32[36,1,18,1,128,128]{5,4,3,2,1,0:T(8,128)} %param.6) | data formatting | bytes 84934656
  59.1 119.6 %all-reduce.6.cloned.1.call-done = bf16[18,6,128,128]{3,2,1,0:T(8,128)(2,1)} async-done(((bf16[18,6,128,128]{3,2,1,0:T(8,128)(2,1)}), bf16[18,6,128,128]{3,2,1,0:T(8,128)(2,1)}) %all-reduce.6.cloned.1.call-update) | async-done | bytes 3538960 | tf_op jit(solution)/shard_map/psum | solution.py:9
  178.7 1055.4 %while.18 = (s32[]{:T(128)}, f32[36,18,128,128]{3,2,1,0:T(8,128)}, s32[]{:T(128)}, f32[6,128,128]{2,1,0:T(8,128)}, bf16[36,6,128,128]{2,3,0,1:T(8,128)(2,1)}, /*...) while((s32[]{:T(128)}, f32[36,18,128,128]{3,2,1,0:T(8,128)}, ...), condition=%wide.region_5.6_spmd.clone.clone, body=%wide.region_1.5_spmd.clone.clone.sunk | while | flops 17217585152 | bytes 122127656 | solution.py:76
  178.7 27.0 %fusion.30 = f32[36,128,128]{1,2,0:T(8,128)S(1)} fusion(f32[36,18,128,128]{3,2,1,0:T(8,128)} %get-tuple-element.557, bf16[18,6,128,128]{3,2,1,0:T(8,128)(2,1)} %get-tuple-element.586, s32[]{:T(128)S(6)} %select_n.384), kind=kOutput, calls=%fused_computation.6.clone.1 | convolution fusion | flops 16308043776 | bytes 45416452 | tf_op jit(solution)/shard_map/while/body/eval_jaxpr/acxy,cyz->axz/dot_general | solution.py:45
  208.1 42.6 %reduce-scatter.2.cloned.1.call-done = f32[36,16,128]{2,0,1:T(8,128)} async-done(((f32[36,128,128]{2,0,1:T(8,128)}), f32[36,16,128]{2,0,1:T(8,128)}) %reduce-scatter.2.cloned.1.call-update) | async-done | bytes 294928 | tf_op jit(solution)/shard_map/while/body/eval_jaxpr/reduce_scatter | solution.py:48
  252.6 29.3 %all-gather.2.cloned.1.call-done = f32[36,128,128]{2,1,0:T(8,128)} async-done(((f32[36,16,128]{2,1,0:T(8,128)}), f32[36,128,128]{2,1,0:T(8,128)}) %all-gather.2.cloned.1.call-update) | async-done | bytes 2359312 | tf_op jit(solution)/shard_map/while/body/eval_jaxpr/all_gather | solution.py:49
  292.3 54.6 %all-reduce.8.cloned.1.call-done = (f32[128,128]{1,0:T(8,128)}, f32[18,128,128]{1,2,0:T(8,128)}) async-done(((f32[128,128]{1,0:T(8,128)}, f32[18,128,128]{1,2,0:T(8,128)}), (f32[128,128]{1,0:T(8,128)}, f32[18,128,128]{1,2,0:T(8,128)})) %all-reduce.8.cloned.1.call-update) | async-done | bytes 1245200 | tf_op jit(solution)/shard_map/while/body/eval_jaxpr/psum | solution.py:55
  383.6 43.1 %reduce-scatter.2.cloned.1.call-done = f32[36,16,128]{2,0,1:T(8,128)} async-done(((f32[36,128,128]{2,0,1:T(8,128)}), f32[36,16,128]{2,0,1:T(8,128)}) %reduce-scatter.2.cloned.1.call-update) | async-done | bytes 294928 | tf_op jit(solution)/shard_map/while/body/eval_jaxpr/reduce_scatter | solution.py:48
  428.6 29.3 %all-gather.2.cloned.1.call-done = f32[36,128,128]{2,1,0:T(8,128)} async-done(((f32[36,16,128]{2,1,0:T(8,128)}), f32[36,128,128]{2,1,0:T(8,128)}) %all-gather.2.cloned.1.call-update) | async-done | bytes 2359312 | tf_op jit(solution)/shard_map/while/body/eval_jaxpr/all_gather | solution.py:49
  468.3 54.6 %all-reduce.8.cloned.1.call-done = (f32[128,128]{1,0:T(8,128)}, f32[18,128,128]{1,2,0:T(8,128)}) async-done(((f32[128,128]{1,0:T(8,128)}, f32[18,128,128]{1,2,0:T(8,128)}), (f32[128,128]{1,0:T(8,128)}, f32[18,128,128]{1,2,0:T(8,128)})) %all-reduce.8.cloned.1.call-update) | async-done | bytes 1245200 | tf_op jit(solution)/shard_map/while/body/eval_jaxpr/psum | solution.py:55
  530.2 27.1 %fusion.30 = f32[36,128,128]{1,2,0:T(8,128)S(1)} fusion(f32[36,18,128,128]{3,2,1,0:T(8,128)} %get-tuple-element.557, bf16[18,6,128,128]{3,2,1,0:T(8,128)(2,1)} %get-tuple-element.586, s32[]{:T(128)S(6)} %select_n.384), kind=kOutput, calls=%fused_computation.6.clone.1 | convolution fusion | flops 16308043776 | bytes 45416452 | tf_op jit(solution)/shard_map/while/body/eval_jaxpr/acxy,cyz->axz/dot_general | solution.py:45
  559.6 43.1 %reduce-scatter.2.cloned.1.call-done = f32[36,16,128]{2,0,1:T(8,128)} async-done(((f32[36,128,128]{2,0,1:T(8,128)}), f32[36,16,128]{2,0,1:T(8,128)}) %reduce-scatter.2.cloned.1.call-update) | async-done | bytes 294928 | tf_op jit(solution)/shard_map/while/body/eval_jaxpr/reduce_scatter | solution.py:48
  604.6 29.3 %all-gather.2.cloned.1.call-done = f32[36,128,128]{2,1,0:T(8,128)} async-done(((f32[36,16,128]{2,1,0:T(8,128)}), f32[36,128,128]{2,1,0:T(8,128)}) %all-gather.2.cloned.1.call-update) | async-done | bytes 2359312 | tf_op jit(solution)/shard_map/while/body/eval_jaxpr/all_gather | solution.py:49
  644.3 54.6 %all-reduce.8.cloned.1.call-done = (f32[128,128]{1,0:T(8,128)}, f32[18,128,128]{1,2,0:T(8,128)}) async-done(((f32[128,128]{1,0:T(8,128)}, f32[18,128,128]{1,2,0:T(8,128)}), (f32[128,128]{1,0:T(8,128)}, f32[18,128,128]{1,2,0:T(8,128)})) %all-reduce.8.cloned.1.call-update) | async-done | bytes 1245200 | tf_op jit(solution)/shard_map/while/body/eval_jaxpr/psum | solution.py:55
  735.6 43.1 %reduce-scatter.2.cloned.1.call-done = f32[36,16,128]{2,0,1:T(8,128)} async-done(((f32[36,128,128]{2,0,1:T(8,128)}), f32[36,16,128]{2,0,1:T(8,128)}) %reduce-scatter.2.cloned.1.call-update) | async-done | bytes 294928 | tf_op jit(solution)/shard_map/while/body/eval_jaxpr/reduce_scatter | solution.py:48
  780.6 29.3 %all-gather.2.cloned.1.call-done = f32[36,128,128]{2,1,0:T(8,128)} async-done(((f32[36,16,128]{2,1,0:T(8,128)}), f32[36,128,128]{2,1,0:T(8,128)}) %all-gather.2.cloned.1.call-update) | async-done | bytes 2359312 | tf_op jit(solution)/shard_map/while/body/eval_jaxpr/all_gather | solution.py:49
  820.2 54.6 %all-reduce.8.cloned.1.call-done = (f32[128,128]{1,0:T(8,128)}, f32[18,128,128]{1,2,0:T(8,128)}) async-done(((f32[128,128]{1,0:T(8,128)}, f32[18,128,128]{1,2,0:T(8,128)}), (f32[128,128]{1,0:T(8,128)}, f32[18,128,128]{1,2,0:T(8,128)})) %all-reduce.8.cloned.1.call-update) | async-done | bytes 1245200 | tf_op jit(solution)/shard_map/while/body/eval_jaxpr/psum | solution.py:55
  882.2 27.0 %fusion.30 = f32[36,128,128]{1,2,0:T(8,128)S(1)} fusion(f32[36,18,128,128]{3,2,1,0:T(8,128)} %get-tuple-element.557, bf16[18,6,128,128]{3,2,1,0:T(8,128)(2,1)} %get-tuple-element.586, s32[]{:T(128)S(6)} %select_n.384), kind=kOutput, calls=%fused_computation.6.clone.1 | convolution fusion | flops 16308043776 | bytes 45416452 | tf_op jit(solution)/shard_map/while/body/eval_jaxpr/acxy,cyz->axz/dot_general | solution.py:45
  911.6 43.1 %reduce-scatter.2.cloned.1.call-done = f32[36,16,128]{2,0,1:T(8,128)} async-done(((f32[36,128,128]{2,0,1:T(8,128)}), f32[36,16,128]{2,0,1:T(8,128)}) %reduce-scatter.2.cloned.1.call-update) | async-done | bytes 294928 | tf_op jit(solution)/shard_map/while/body/eval_jaxpr/reduce_scatter | solution.py:48
  956.5 29.3 %all-gather.2.cloned.1.call-done = f32[36,128,128]{2,1,0:T(8,128)} async-done(((f32[36,16,128]{2,1,0:T(8,128)}), f32[36,128,128]{2,1,0:T(8,128)}) %all-gather.2.cloned.1.call-update) | async-done | bytes 2359312 | tf_op jit(solution)/shard_map/while/body/eval_jaxpr/all_gather | solution.py:49
  996.2 54.6 %all-reduce.8.cloned.1.call-done = (f32[128,128]{1,0:T(8,128)}, f32[18,128,128]{1,2,0:T(8,128)}) async-done(((f32[128,128]{1,0:T(8,128)}, f32[18,128,128]{1,2,0:T(8,128)}), (f32[128,128]{1,0:T(8,128)}, f32[18,128,128]{1,2,0:T(8,128)})) %all-reduce.8.cloned.1.call-update) | async-done | bytes 1245200 | tf_op jit(solution)/shard_map/while/body/eval_jaxpr/psum | solution.py:55
  1087.5 43.1 %reduce-scatter.2.cloned.1.call-done = f32[36,16,128]{2,0,1:T(8,128)} async-done(((f32[36,128,128]{2,0,1:T(8,128)}), f32[36,16,128]{2,0,1:T(8,128)}) %reduce-scatter.2.cloned.1.call-update) | async-done | bytes 294928 | tf_op jit(solution)/shard_map/while/body/eval_jaxpr/reduce_scatter | solution.py:48
  1132.5 29.3 %all-gather.2.cloned.1.call-done = f32[36,128,128]{2,1,0:T(8,128)} async-done(((f32[36,16,128]{2,1,0:T(8,128)}), f32[36,128,128]{2,1,0:T(8,128)}) %all-gather.2.cloned.1.call-update) | async-done | bytes 2359312 | tf_op jit(solution)/shard_map/while/body/eval_jaxpr/all_gather | solution.py:49
  1172.2 54.6 %all-reduce.8.cloned.1.call-done = (f32[128,128]{1,0:T(8,128)}, f32[18,128,128]{1,2,0:T(8,128)}) async-done(((f32[128,128]{1,0:T(8,128)}, f32[18,128,128]{1,2,0:T(8,128)}), (f32[128,128]{1,0:T(8,128)}, f32[18,128,128]{1,2,0:T(8,128)})) %all-reduce.8.cloned.1.call-update) | async-done | bytes 1245200 | tf_op jit(solution)/shard_map/while/body/eval_jaxpr/psum | solution.py:55
  (176 shorter events, 234.0 us)
Async XLA Ops:
  6.5 172.2 %all-reduce.6.cloned.1.call-start = ((), (), s32[]{:S(2)}) async-start(), calls=%async_computation.1 | async-start | bytes 7077888 | tf_op jit(solution)/shard_map/psum | solution.py:9
  178.7 72.0 %reduce-scatter.2.cloned.1.call-start = ((), (), s32[]{:S(2)}) async-start(), calls=%async_computation.2 | async-start | bytes 2949120 | tf_op jit(solution)/shard_map/while/body/eval_jaxpr/reduce_scatter | solution.py:48
  208.1 73.9 %all-gather.2.cloned.1.call-start = ((), (), s32[]{:S(2)}) async-start(), calls=%async_computation.3 | async-start | bytes 2654208 | tf_op jit(solution)/shard_map/while/body/eval_jaxpr/all_gather | solution.py:49
  252.5 94.4 %all-reduce.8.cloned.1.call-start = ((), (), s32[]{:S(2)}) async-start(), calls=%async_computation.4 | async-start | bytes 2490368 | tf_op jit(solution)/shard_map/while/body/eval_jaxpr/psum | solution.py:55
  288.8 59.1 %copy-start.2 = (f32[36,128,128]{2,1,0:T(8,128)S(1)}, f32[36,128,128]{2,1,0:T(8,128)}, u32[]{:S(2)}) copy-start(f32[36,128,128]{2,1,0:T(8,128)} %all-gather.2.cloned.1.call-done) | copy-start | bytes 7077892 | tf_op jit(solution)/shard_map/while
  354.2 72.5 %reduce-scatter.2.cloned.1.call-start = ((), (), s32[]{:S(2)}) async-start(), calls=%async_computation.2 | async-start | bytes 2949120 | tf_op jit(solution)/shard_map/while/body/eval_jaxpr/reduce_scatter | solution.py:48
  383.6 74.3 %all-gather.2.cloned.1.call-start = ((), (), s32[]{:S(2)}) async-start(), calls=%async_computation.3 | async-start | bytes 2654208 | tf_op jit(solution)/shard_map/while/body/eval_jaxpr/all_gather | solution.py:49
  428.5 94.4 %all-reduce.8.cloned.1.call-start = ((), (), s32[]{:S(2)}) async-start(), calls=%async_computation.4 | async-start | bytes 2490368 | tf_op jit(solution)/shard_map/while/body/eval_jaxpr/psum | solution.py:55
  464.8 59.1 %copy-start.2 = (f32[36,128,128]{2,1,0:T(8,128)S(1)}, f32[36,128,128]{2,1,0:T(8,128)}, u32[]{:S(2)}) copy-start(f32[36,128,128]{2,1,0:T(8,128)} %all-gather.2.cloned.1.call-done) | copy-start | bytes 7077892 | tf_op jit(solution)/shard_map/while
  530.2 72.5 %reduce-scatter.2.cloned.1.call-start = ((), (), s32[]{:S(2)}) async-start(), calls=%async_computation.2 | async-start | bytes 2949120 | tf_op jit(solution)/shard_map/while/body/eval_jaxpr/reduce_scatter | solution.py:48
  559.6 74.3 %all-gather.2.cloned.1.call-start = ((), (), s32[]{:S(2)}) async-start(), calls=%async_computation.3 | async-start | bytes 2654208 | tf_op jit(solution)/shard_map/while/body/eval_jaxpr/all_gather | solution.py:49
  604.5 94.4 %all-reduce.8.cloned.1.call-start = ((), (), s32[]{:S(2)}) async-start(), calls=%async_computation.4 | async-start | bytes 2490368 | tf_op jit(solution)/shard_map/while/body/eval_jaxpr/psum | solution.py:55
  640.8 59.1 %copy-start.2 = (f32[36,128,128]{2,1,0:T(8,128)S(1)}, f32[36,128,128]{2,1,0:T(8,128)}, u32[]{:S(2)}) copy-start(f32[36,128,128]{2,1,0:T(8,128)} %all-gather.2.cloned.1.call-done) | copy-start | bytes 7077892 | tf_op jit(solution)/shard_map/while
  706.2 72.5 %reduce-scatter.2.cloned.1.call-start = ((), (), s32[]{:S(2)}) async-start(), calls=%async_computation.2 | async-start | bytes 2949120 | tf_op jit(solution)/shard_map/while/body/eval_jaxpr/reduce_scatter | solution.py:48
  735.6 74.3 %all-gather.2.cloned.1.call-start = ((), (), s32[]{:S(2)}) async-start(), calls=%async_computation.3 | async-start | bytes 2654208 | tf_op jit(solution)/shard_map/while/body/eval_jaxpr/all_gather | solution.py:49
  780.5 94.4 %all-reduce.8.cloned.1.call-start = ((), (), s32[]{:S(2)}) async-start(), calls=%async_computation.4 | async-start | bytes 2490368 | tf_op jit(solution)/shard_map/while/body/eval_jaxpr/psum | solution.py:55
  816.8 59.1 %copy-start.2 = (f32[36,128,128]{2,1,0:T(8,128)S(1)}, f32[36,128,128]{2,1,0:T(8,128)}, u32[]{:S(2)}) copy-start(f32[36,128,128]{2,1,0:T(8,128)} %all-gather.2.cloned.1.call-done) | copy-start | bytes 7077892 | tf_op jit(solution)/shard_map/while
  882.2 72.5 %reduce-scatter.2.cloned.1.call-start = ((), (), s32[]{:S(2)}) async-start(), calls=%async_computation.2 | async-start | bytes 2949120 | tf_op jit(solution)/shard_map/while/body/eval_jaxpr/reduce_scatter | solution.py:48
  911.5 74.3 %all-gather.2.cloned.1.call-start = ((), (), s32[]{:S(2)}) async-start(), calls=%async_computation.3 | async-start | bytes 2654208 | tf_op jit(solution)/shard_map/while/body/eval_jaxpr/all_gather | solution.py:49
  956.5 94.4 %all-reduce.8.cloned.1.call-start = ((), (), s32[]{:S(2)}) async-start(), calls=%async_computation.4 | async-start | bytes 2490368 | tf_op jit(solution)/shard_map/while/body/eval_jaxpr/psum | solution.py:55
  992.7 59.1 %copy-start.2 = (f32[36,128,128]{2,1,0:T(8,128)S(1)}, f32[36,128,128]{2,1,0:T(8,128)}, u32[]{:S(2)}) copy-start(f32[36,128,128]{2,1,0:T(8,128)} %all-gather.2.cloned.1.call-done) | copy-start | bytes 7077892 | tf_op jit(solution)/shard_map/while
  1058.2 72.5 %reduce-scatter.2.cloned.1.call-start = ((), (), s32[]{:S(2)}) async-start(), calls=%async_computation.2 | async-start | bytes 2949120 | tf_op jit(solution)/shard_map/while/body/eval_jaxpr/reduce_scatter | solution.py:48
  1087.5 74.3 %all-gather.2.cloned.1.call-start = ((), (), s32[]{:S(2)}) async-start(), calls=%async_computation.3 | async-start | bytes 2654208 | tf_op jit(solution)/shard_map/while/body/eval_jaxpr/all_gather | solution.py:49
  1132.4 94.4 %all-reduce.8.cloned.1.call-start = ((), (), s32[]{:S(2)}) async-start(), calls=%async_computation.4 | async-start | bytes 2490368 | tf_op jit(solution)/shard_map/while/body/eval_jaxpr/psum | solution.py:55
  (9 other events, 100.3 us)
Sparse Core Ops, SparseCore 0:
  42.2 136.4 all-reduce.5
  208.2 42.5 reduce-scatter.1
  252.6 29.2 all-gather.1
  288.8 58.0 all-reduce.7
  383.7 42.9 reduce-scatter.1
  428.6 29.2 all-gather.1
  464.8 58.0 all-reduce.7
  559.7 42.9 reduce-scatter.1
  604.6 29.2 all-gather.1
  640.8 58.0 all-reduce.7
  735.7 42.9 reduce-scatter.1
  780.6 29.2 all-gather.1
  816.8 58.0 all-reduce.7
  911.6 42.9 reduce-scatter.1
  956.6 29.2 all-gather.1
  992.8 58.0 all-reduce.7
  1087.6 42.9 reduce-scatter.1
  1132.5 29.2 all-gather.1
  1168.7 58.0 all-reduce.7
where the time goes:
time: 1240 us
  waiting for transfers between devices  882 us (71%)
  matrix products  182 us (15%)
  local copies, waits for them, and re-layouts  101 us (8%)
  other arithmetic  62.3 us (5%)
  between operations  13.1 us (1%)
    psum x6, waiting for transfers between devices, advance(): diag_total = lax.psum(diag_term, 'prow')  328 us
    reduce_scatter x6, waiting for transfers between devices, advance(): lax.psum_scatter(partial_value, 'pcol', scatter_dimension=1, tiled=True)  258 us
    all_gather x6, waiting for transfers between devices, advance(): col_whole = lax.all_gather(col_piece, 'pcol', axis=1, tiled=True)  176 us
    dot_general x6, matrix products, advance(): jnp.einsum('acxy,cyz->axz', matrix, other_rows.astype(jnp.float32), preci...  162 us
    psum x1, waiting for transfers between devices, spread(): return lax.psum(kept, axis)  120 us
    unnamed x7, local copies, waits for them, and re-layouts  41.9 us
  transfers between devices with their start and end apart: 19, of which 19 were waited for; matrix products, arithmetic and copies ran while one was open for 3% of the time, Pallas kernels for 0%

commit v1 on v0

--- a/solution.py
+++ b/solution.py
@@ -52,7 +52,8 @@
         diag_term = jnp.einsum(
             "axy,axz->yz", own_col.astype(jnp.float32), inverse_col, precision=lax.Precision.HIGHEST
         )
-        diag_total = lax.psum(diag_term, "prow")
+        shards = lax.all_gather(diag_term, "prow")
+        diag_total = jnp.sum(shards, axis=0)
         diag_block = lax.dynamic_index_in_dim(dinv, column, 0, keepdims=False) - diag_total
         new_col = jnp.where((row_ids == column)[:, None, None], diag_block[None], inverse_col)
         col_slot = column // col_count

time: 1240 us -> 1230 us (level)
  waiting for transfers between devices: 882 us -> 739 us
  blocking collectives: 0 us -> 95.7 us
  other arithmetic: 62.3 us -> 82 us
  local copies, waits for them, and re-layouts: 101 us -> 118 us
    psum x6 -> x0, waiting for transfers between devices: 328 us -> none  [advance(): diag_total = lax.psum(diag_term, 'prow')]
    psum x1 -> x7, waiting for transfers between devices: 120 us -> 325 us  [spread(): return lax.psum(kept, axis)]
    all_gather x0 -> x6, blocking collectives: none -> 95.7 us  [advance(): shards = lax.all_gather(diag_term, 'prow')]
    all_gather x6, waiting for transfers between devices: 176 us -> 155 us  [advance(): col_whole = lax.all_gather(col_piece, 'pcol', axis=1, tiled=True)]
    while x30 -> x6, local copies, waits for them, and re-layouts: 3.15 us -> 16 us
  transfers between devices with their start and end apart: 19 -> 19, of which waited for: 19 -> 19; matrix products, arithmetic and copies ran while one was open for 3% -> 8% of each run, Pallas kernels for 0% -> 0%
where the time goes in v1:
time: 1230 us
  waiting for transfers between devices  739 us (60%)
  matrix products  178 us (14%)
  local copies, waits for them, and re-layouts  118 us (10%)
  blocking collectives  95.7 us (8%)
  other arithmetic  82 us (7%)
  between operations  13.1 us (1%)
    psum x7, waiting for transfers between devices, spread(): return lax.psum(kept, axis)  325 us
    reduce_scatter x6, waiting for transfers between devices, advance(): lax.psum_scatter(partial_value, 'pcol', scatter_dimension=1, tiled=True)  258 us
    dot_general x6, matrix products, advance(): jnp.einsum('acxy,cyz->axz', matrix, other_rows.astype(jnp.float32), preci...  162 us
    all_gather x6, waiting for transfers between devices, advance(): col_whole = lax.all_gather(col_piece, 'pcol', axis=1, tiled=True)  155 us
    all_gather x6, blocking collectives, advance(): shards = lax.all_gather(diag_term, 'prow')  95.7 us
    unnamed x7, local copies, waits for them, and re-layouts  42 us
    dynamic_update_slice x6, other arithmetic, advance(): lax.dynamic_update_index_in_dim(matrix, jnp.where(pcol_id == column % col...  25.3 us
  transfers between devices with their start and end apart: 19, of which 19 were waited for; matrix products, arithmetic and copies ran while one was open for 8% of the time, Pallas kernels for 0%

profile of v1, /device:TPU:0, one launch (start us, length us, event | category | flops | bytes accessed | tf_op | source)
XLA Modules:
  0.0 1226.8 jit_solution(9912525630681480986)
XLA Ops:
  6.5 30.5 %copy.54 = f32[36,1,18,1,128,128]{5,4,3,2,1,0:T(8,128)} copy(f32[36,1,18,1,128,128]{5,4,3,2,1,0:T(8,128)} %param.6) | data formatting | bytes 84934656
  59.2 119.5 %all-reduce.3.cloned.1.call-done = bf16[18,6,128,128]{3,2,1,0:T(8,128)(2,1)} async-done(((bf16[18,6,128,128]{3,2,1,0:T(8,128)(2,1)}), bf16[18,6,128,128]{3,2,1,0:T(8,128)(2,1)}) %all-reduce.3.cloned.1.call-update) | async-done | bytes 3538960 | tf_op jit(solution)/shard_map/psum | solution.py:9
  178.7 1040.6 %while.18 = (s32[]{:T(128)}, f32[36,18,128,128]{3,2,1,0:T(8,128)}, s32[]{:T(128)}, f32[6,128,128]{2,1,0:T(8,128)}, bf16[36,6,128,128]{2,3,0,1:T(8,128)(2,1)}, /*...) while((s32[]{:T(128)}, f32[36,18,128,128]{3,2,1,0:T(8,128)}, ...), condition=%wide.region_5.6_spmd.clone.clone, body=%wide.region_1.5_spmd.clone.clone.sunk | while | flops 17217617920 | bytes 108233968 | solution.py:77
  178.7 27.0 %fusion.32 = f32[36,128,128]{1,2,0:T(8,128)S(1)} fusion(f32[36,18,128,128]{3,2,1,0:T(8,128)} %get-tuple-element.552, bf16[18,6,128,128]{3,2,1,0:T(8,128)(2,1)} %get-tuple-element.582, s32[]{:T(128)S(6)} %select_n.384), kind=kOutput, calls=%fused_computation.6.clone.1 | convolution fusion | flops 16308043776 | bytes 45416452 | tf_op jit(solution)/shard_map/while/body/eval_jaxpr/acxy,cyz->axz/dot_general | solution.py:45
  208.0 42.6 %reduce-scatter.2.cloned.1.call-done = f32[36,16,128]{2,0,1:T(8,128)} async-done(((f32[36,128,128]{2,0,1:T(8,128)}), f32[36,16,128]{2,0,1:T(8,128)}) %reduce-scatter.2.cloned.1.call-update) | async-done | bytes 294928 | tf_op jit(solution)/shard_map/while/body/eval_jaxpr/reduce_scatter | solution.py:48
  315.1 34.2 %all-reduce.5.cloned.1.call-done = f32[18,128,128]{1,2,0:T(8,128)} async-done(((f32[18,128,128]{1,2,0:T(8,128)}), f32[18,128,128]{1,2,0:T(8,128)}) %all-reduce.5.cloned.1.call-update) | async-done | bytes 1179664 | tf_op jit(solution)/shard_map/while/body/eval_jaxpr/psum | solution.py:9
  351.8 27.0 %fusion.32 = f32[36,128,128]{1,2,0:T(8,128)S(1)} fusion(f32[36,18,128,128]{3,2,1,0:T(8,128)} %get-tuple-element.552, bf16[18,6,128,128]{3,2,1,0:T(8,128)(2,1)} %get-tuple-element.582, s32[]{:T(128)S(6)} %select_n.384), kind=kOutput, calls=%fused_computation.6.clone.1 | convolution fusion | flops 16308043776 | bytes 45416452 | tf_op jit(solution)/shard_map/while/body/eval_jaxpr/acxy,cyz->axz/dot_general | solution.py:45
  381.0 43.0 %reduce-scatter.2.cloned.1.call-done = f32[36,16,128]{2,0,1:T(8,128)} async-done(((f32[36,128,128]{2,0,1:T(8,128)}), f32[36,16,128]{2,0,1:T(8,128)}) %reduce-scatter.2.cloned.1.call-update) | async-done | bytes 294928 | tf_op jit(solution)/shard_map/while/body/eval_jaxpr/reduce_scatter | solution.py:48
  429.4 25.9 %all-gather.7.cloned.1.call-done = f32[36,128,128]{2,1,0:T(8,128)} async-done(((f32[36,16,128]{2,1,0:T(8,128)}), f32[36,128,128]{2,1,0:T(8,128)}) %all-gather.7.cloned.1.call-update) | async-done | bytes 2359312 | tf_op jit(solution)/shard_map/while/body/eval_jaxpr/all_gather | solution.py:49
  488.6 34.2 %all-reduce.5.cloned.1.call-done = f32[18,128,128]{1,2,0:T(8,128)} async-done(((f32[18,128,128]{1,2,0:T(8,128)}), f32[18,128,128]{1,2,0:T(8,128)}) %all-reduce.5.cloned.1.call-update) | async-done | bytes 1179664 | tf_op jit(solution)/shard_map/while/body/eval_jaxpr/psum | solution.py:9
  525.3 27.0 %fusion.32 = f32[36,128,128]{1,2,0:T(8,128)S(1)} fusion(f32[36,18,128,128]{3,2,1,0:T(8,128)} %get-tuple-element.552, bf16[18,6,128,128]{3,2,1,0:T(8,128)(2,1)} %get-tuple-element.582, s32[]{:T(128)S(6)} %select_n.384), kind=kOutput, calls=%fused_computation.6.clone.1 | convolution fusion | flops 16308043776 | bytes 45416452 | tf_op jit(solution)/shard_map/while/body/eval_jaxpr/acxy,cyz->axz/dot_general | solution.py:45
  554.6 43.0 %reduce-scatter.2.cloned.1.call-done = f32[36,16,128]{2,0,1:T(8,128)} async-done(((f32[36,128,128]{2,0,1:T(8,128)}), f32[36,16,128]{2,0,1:T(8,128)}) %reduce-scatter.2.cloned.1.call-update) | async-done | bytes 294928 | tf_op jit(solution)/shard_map/while/body/eval_jaxpr/reduce_scatter | solution.py:48
  662.1 34.2 %all-reduce.5.cloned.1.call-done = f32[18,128,128]{1,2,0:T(8,128)} async-done(((f32[18,128,128]{1,2,0:T(8,128)}), f32[18,128,128]{1,2,0:T(8,128)}) %all-reduce.5.cloned.1.call-update) | async-done | bytes 1179664 | tf_op jit(solution)/shard_map/while/body/eval_jaxpr/psum | solution.py:9
  698.8 27.0 %fusion.32 = f32[36,128,128]{1,2,0:T(8,128)S(1)} fusion(f32[36,18,128,128]{3,2,1,0:T(8,128)} %get-tuple-element.552, bf16[18,6,128,128]{3,2,1,0:T(8,128)(2,1)} %get-tuple-element.582, s32[]{:T(128)S(6)} %select_n.384), kind=kOutput, calls=%fused_computation.6.clone.1 | convolution fusion | flops 16308043776 | bytes 45416452 | tf_op jit(solution)/shard_map/while/body/eval_jaxpr/acxy,cyz->axz/dot_general | solution.py:45
  728.1 43.0 %reduce-scatter.2.cloned.1.call-done = f32[36,16,128]{2,0,1:T(8,128)} async-done(((f32[36,128,128]{2,0,1:T(8,128)}), f32[36,16,128]{2,0,1:T(8,128)}) %reduce-scatter.2.cloned.1.call-update) | async-done | bytes 294928 | tf_op jit(solution)/shard_map/while/body/eval_jaxpr/reduce_scatter | solution.py:48
  776.4 25.9 %all-gather.7.cloned.1.call-done = f32[36,128,128]{2,1,0:T(8,128)} async-done(((f32[36,16,128]{2,1,0:T(8,128)}), f32[36,128,128]{2,1,0:T(8,128)}) %all-gather.7.cloned.1.call-update) | async-done | bytes 2359312 | tf_op jit(solution)/shard_map/while/body/eval_jaxpr/all_gather | solution.py:49
  835.6 34.2 %all-reduce.5.cloned.1.call-done = f32[18,128,128]{1,2,0:T(8,128)} async-done(((f32[18,128,128]{1,2,0:T(8,128)}), f32[18,128,128]{1,2,0:T(8,128)}) %all-reduce.5.cloned.1.call-update) | async-done | bytes 1179664 | tf_op jit(solution)/shard_map/while/body/eval_jaxpr/psum | solution.py:9
  872.3 27.1 %fusion.32 = f32[36,128,128]{1,2,0:T(8,128)S(1)} fusion(f32[36,18,128,128]{3,2,1,0:T(8,128)} %get-tuple-element.552, bf16[18,6,128,128]{3,2,1,0:T(8,128)(2,1)} %get-tuple-element.582, s32[]{:T(128)S(6)} %select_n.384), kind=kOutput, calls=%fused_computation.6.clone.1 | convolution fusion | flops 16308043776 | bytes 45416452 | tf_op jit(solution)/shard_map/while/body/eval_jaxpr/acxy,cyz->axz/dot_general | solution.py:45
  901.6 43.0 %reduce-scatter.2.cloned.1.call-done = f32[36,16,128]{2,0,1:T(8,128)} async-done(((f32[36,128,128]{2,0,1:T(8,128)}), f32[36,16,128]{2,0,1:T(8,128)}) %reduce-scatter.2.cloned.1.call-update) | async-done | bytes 294928 | tf_op jit(solution)/shard_map/while/body/eval_jaxpr/reduce_scatter | solution.py:48
  1009.2 34.2 %all-reduce.5.cloned.1.call-done = f32[18,128,128]{1,2,0:T(8,128)} async-done(((f32[18,128,128]{1,2,0:T(8,128)}), f32[18,128,128]{1,2,0:T(8,128)}) %all-reduce.5.cloned.1.call-update) | async-done | bytes 1179664 | tf_op jit(solution)/shard_map/while/body/eval_jaxpr/psum | solution.py:9
  1045.9 27.0 %fusion.32 = f32[36,128,128]{1,2,0:T(8,128)S(1)} fusion(f32[36,18,128,128]{3,2,1,0:T(8,128)} %get-tuple-element.552, bf16[18,6,128,128]{3,2,1,0:T(8,128)(2,1)} %get-tuple-element.582, s32[]{:T(128)S(6)} %select_n.384), kind=kOutput, calls=%fused_computation.6.clone.1 | convolution fusion | flops 16308043776 | bytes 45416452 | tf_op jit(solution)/shard_map/while/body/eval_jaxpr/acxy,cyz->axz/dot_general | solution.py:45
  1075.1 43.0 %reduce-scatter.2.cloned.1.call-done = f32[36,16,128]{2,0,1:T(8,128)} async-done(((f32[36,128,128]{2,0,1:T(8,128)}), f32[36,16,128]{2,0,1:T(8,128)}) %reduce-scatter.2.cloned.1.call-update) | async-done | bytes 294928 | tf_op jit(solution)/shard_map/while/body/eval_jaxpr/reduce_scatter | solution.py:48
  1123.4 25.9 %all-gather.7.cloned.1.call-done = f32[36,128,128]{2,1,0:T(8,128)} async-done(((f32[36,16,128]{2,1,0:T(8,128)}), f32[36,128,128]{2,1,0:T(8,128)}) %all-gather.7.cloned.1.call-update) | async-done | bytes 2359312 | tf_op jit(solution)/shard_map/while/body/eval_jaxpr/all_gather | solution.py:49
  1182.6 34.2 %all-reduce.5.cloned.1.call-done = f32[18,128,128]{1,2,0:T(8,128)} async-done(((f32[18,128,128]{1,2,0:T(8,128)}), f32[18,128,128]{1,2,0:T(8,128)}) %all-reduce.5.cloned.1.call-update) | async-done | bytes 1179664 | tf_op jit(solution)/shard_map/while/body/eval_jaxpr/psum | solution.py:9
  (164 shorter events, 359.4 us)
Async XLA Ops:
  6.5 30.6 %copy-start = (s32[144,144]{1,0:T(8,128)S(1)}, s32[144,144]{1,0:T(8,128)}, u32[]{:S(2)}) copy-start(s32[144,144]{1,0:T(8,128)} %param.9) | copy-start | bytes 248836
  6.5 172.2 %all-reduce.3.cloned.1.call-start = ((), (), s32[]{:S(2)}) async-start(), calls=%async_computation.1 | async-start | bytes 7077888 | tf_op jit(solution)/shard_map/psum | solution.py:9
  178.7 71.9 %reduce-scatter.2.cloned.1.call-start = ((), (), s32[]{:S(2)}) async-start(), calls=%async_computation.2 | async-start | bytes 2949120 | tf_op jit(solution)/shard_map/while/body/eval_jaxpr/reduce_scatter | solution.py:48
  208.0 73.8 %all-gather.7.cloned.1.call-start = ((), (), s32[]{:S(2)}) async-start(), calls=%async_computation.3 | async-start | bytes 2654208 | tf_op jit(solution)/shard_map/while/body/eval_jaxpr/all_gather | solution.py:49
  252.4 96.9 %all-reduce.5.cloned.1.call-start = ((), (), s32[]{:S(2)}) async-start(), calls=%async_computation.4 | async-start | bytes 2359296 | tf_op jit(solution)/shard_map/while/body/eval_jaxpr/psum | solution.py:9
  351.8 72.3 %reduce-scatter.2.cloned.1.call-start = ((), (), s32[]{:S(2)}) async-start(), calls=%async_computation.2 | async-start | bytes 2949120 | tf_op jit(solution)/shard_map/while/body/eval_jaxpr/reduce_scatter | solution.py:48
  381.0 74.3 %all-gather.7.cloned.1.call-start = ((), (), s32[]{:S(2)}) async-start(), calls=%async_computation.3 | async-start | bytes 2654208 | tf_op jit(solution)/shard_map/while/body/eval_jaxpr/all_gather | solution.py:49
  425.9 96.9 %all-reduce.5.cloned.1.call-start = ((), (), s32[]{:S(2)}) async-start(), calls=%async_computation.4 | async-start | bytes 2359296 | tf_op jit(solution)/shard_map/while/body/eval_jaxpr/psum | solution.py:9
  525.3 72.3 %reduce-scatter.2.cloned.1.call-start = ((), (), s32[]{:S(2)}) async-start(), calls=%async_computation.2 | async-start | bytes 2949120 | tf_op jit(solution)/shard_map/while/body/eval_jaxpr/reduce_scatter | solution.py:48
  554.5 74.3 %all-gather.7.cloned.1.call-start = ((), (), s32[]{:S(2)}) async-start(), calls=%async_computation.3 | async-start | bytes 2654208 | tf_op jit(solution)/shard_map/while/body/eval_jaxpr/all_gather | solution.py:49
  599.4 96.9 %all-reduce.5.cloned.1.call-start = ((), (), s32[]{:S(2)}) async-start(), calls=%async_computation.4 | async-start | bytes 2359296 | tf_op jit(solution)/shard_map/while/body/eval_jaxpr/psum | solution.py:9
  698.8 72.3 %reduce-scatter.2.cloned.1.call-start = ((), (), s32[]{:S(2)}) async-start(), calls=%async_computation.2 | async-start | bytes 2949120 | tf_op jit(solution)/shard_map/while/body/eval_jaxpr/reduce_scatter | solution.py:48
  728.0 74.3 %all-gather.7.cloned.1.call-start = ((), (), s32[]{:S(2)}) async-start(), calls=%async_computation.3 | async-start | bytes 2654208 | tf_op jit(solution)/shard_map/while/body/eval_jaxpr/all_gather | solution.py:49
  772.9 96.9 %all-reduce.5.cloned.1.call-start = ((), (), s32[]{:S(2)}) async-start(), calls=%async_computation.4 | async-start | bytes 2359296 | tf_op jit(solution)/shard_map/while/body/eval_jaxpr/psum | solution.py:9
  872.3 72.4 %reduce-scatter.2.cloned.1.call-start = ((), (), s32[]{:S(2)}) async-start(), calls=%async_computation.2 | async-start | bytes 2949120 | tf_op jit(solution)/shard_map/while/body/eval_jaxpr/reduce_scatter | solution.py:48
  901.6 74.3 %all-gather.7.cloned.1.call-start = ((), (), s32[]{:S(2)}) async-start(), calls=%async_computation.3 | async-start | bytes 2654208 | tf_op jit(solution)/shard_map/while/body/eval_jaxpr/all_gather | solution.py:49
  946.5 96.9 %all-reduce.5.cloned.1.call-start = ((), (), s32[]{:S(2)}) async-start(), calls=%async_computation.4 | async-start | bytes 2359296 | tf_op jit(solution)/shard_map/while/body/eval_jaxpr/psum | solution.py:9
  1045.9 72.3 %reduce-scatter.2.cloned.1.call-start = ((), (), s32[]{:S(2)}) async-start(), calls=%async_computation.2 | async-start | bytes 2949120 | tf_op jit(solution)/shard_map/while/body/eval_jaxpr/reduce_scatter | solution.py:48
  1075.1 74.3 %all-gather.7.cloned.1.call-start = ((), (), s32[]{:S(2)}) async-start(), calls=%async_computation.3 | async-start | bytes 2654208 | tf_op jit(solution)/shard_map/while/body/eval_jaxpr/all_gather | solution.py:49
  1119.9 96.9 %all-reduce.5.cloned.1.call-start = ((), (), s32[]{:S(2)}) async-start(), calls=%async_computation.4 | async-start | bytes 2359296 | tf_op jit(solution)/shard_map/while/body/eval_jaxpr/psum | solution.py:9
  1219.4 0.9 copy-start.1
Sparse Core Ops, SparseCore 0:
  42.2 136.4 all-reduce.2
  208.1 42.4 reduce-scatter.1
  252.5 29.2 all-gather.6
  290.0 59.2 all-reduce.4
  381.1 42.9 reduce-scatter.1
  426.0 29.2 all-gather.6
  463.5 59.2 all-reduce.4
  554.6 42.9 reduce-scatter.1
  599.5 29.2 all-gather.6
  637.0 59.2 all-reduce.4
  728.1 42.9 reduce-scatter.1
  773.0 29.2 all-gather.6
  810.5 59.2 all-reduce.4
  901.7 42.9 reduce-scatter.1
  946.6 29.2 all-gather.6
  984.1 59.2 all-reduce.4
  1075.2 42.9 reduce-scatter.1
  1120.1 29.2 all-gather.6
  1157.6 59.2 all-reduce.4
